TPU v7x, 512 devices: a whole 4x4x16 slice. The times are simulated.
512 devices in a mesh: dom: 64 (over z, y), rep: 8 (over x, core).
Axes of the slice: x: 4, y: 4, z: 16, core: 2. Of those that a mesh axis runs over, the one named last changes fastest.
Arguments:
- feats: bfloat16 [65536, 128], P(('dom', 'rep')), may hold values from -6 to 6
- weight: bfloat16 [128, 128], replicated, may hold values from -0.5 to 0.5
- bias: float32 [128], replicated, may hold values from -3 to 3
- tiles: bfloat16 [512, 5, 28, 128, 128], P(('dom', 'rep')), may hold values from -0.0625 to 0.0625
- tile_cols: int32 [512, 5, 28], P(('dom', 'rep')), may hold values from 0 to 7
- tile_count: int32 [512, 5], P(('dom', 'rep')), may hold values from 2 to 28, as said below
- cotangent: bfloat16 [65536, 128], P(('dom', 'rep')), may hold values from -6 to 6
Outputs:
- hidden: bfloat16 [65536, 128], P(('dom', 'rep'))
- grad_weight: float32 [128, 128], replicated
- grad_bias: float32 [128], replicated
- grad_feats: bfloat16 [65536, 128], P(('dom', 'rep'))
Inputs may be any that keep to these rules, and one draw needn't show every extreme that they name: `tile_count`: every list has at least two live tiles; the nodes of some device have 28 live tiles in every list, and those of most devices far fewer.
All inputs are finite; a program needn't handle non-finite values.
Results may differ from a plain program's by a relative error of at most 0.0062.
Values may be sent and summed in bfloat16 or wider, within the bound.
A program may use at most 64 MiB of HBM per device.

v0:
```python
import jax
import jax.numpy as jnp
from jax import lax
from jax.sharding import PartitionSpec as P


def swapped(value, axis, bit):
    mask = 2**bit
    pairs = [(source, source ^ mask) for source in range(lax.axis_size(axis))]
    return lax.ppermute(value, axis, pairs)


def gelu_tanh(values):
    return jax.nn.gelu(values, approximate=True)


def add_slot(summed, panel, slot, tiles, tile_cols, live_mask):
    tgt_blocks, slot_count, max_tiles, block, unused = tiles.shape
    width = panel.shape[1]
    panel_blocks = panel.shape[0] // block
    source = panel.reshape(panel_blocks, block, width)
    columns = tile_cols[:, slot]
    slot_tiles = tiles[:, slot]
    fetched = source[columns]
    fetched = jnp.where(live_mask[:, slot][:, :, None, None], fetched, jnp.zeros((), jnp.bfloat16))
    return summed + jnp.einsum(
        "tmij,tmjh->tih", slot_tiles, fetched, preferred_element_type=jnp.float32
    )


def partial_panel(slot, tiles, tile_cols, live_mask, grad_rows_b, panel_blocks):
    tgt_blocks, slot_count, max_tiles, block, unused = tiles.shape
    width = grad_rows_b.shape[2]
    masked = jnp.where(
        live_mask[:, slot][:, :, None, None], tiles[:, slot], jnp.zeros((), jnp.bfloat16)
    )
    contrib = jnp.einsum("tmij,tih->tmjh", masked, grad_rows_b, preferred_element_type=jnp.float32)
    targets = tile_cols[:, slot].reshape(tgt_blocks * max_tiles)
    placed = jnp.zeros((panel_blocks, block, width), jnp.float32)
    placed = placed.at[targets].add(contrib.reshape(tgt_blocks * max_tiles, block, width))
    return placed.reshape(panel_blocks * block, width)


def body(feats, weight, bias, tiles, tile_cols, tile_count, cotangent):
    dom_size = lax.axis_size("dom")
    rep_size = lax.axis_size("rep")
    top_bit = dom_size.bit_length() - 1
    tgt_blocks, slot_count, max_tiles, block, unused = tiles.shape
    width = weight.shape[1]
    panel_blocks = rep_size * tgt_blocks
    live_mask = jnp.arange(max_tiles)[None, None, :] < tile_count[:, :, None]
    projected = jnp.dot(feats, weight, preferred_element_type=jnp.float32).astype(jnp.bfloat16)
    own_rows = lax.all_gather(projected, "rep", axis=0, tiled=True)
    summed = jnp.zeros((tgt_blocks, block, width), jnp.float32)
    summed = add_slot(summed, own_rows, 0, tiles, tile_cols, live_mask)
    for round_index in range(1, slot_count):
        bit_number = top_bit - round_index
        partner_rows = swapped(own_rows, "dom", bit_number)
        summed = add_slot(summed, partner_rows, round_index, tiles, tile_cols, live_mask)
    preact = summed.reshape(tgt_blocks * block, width) + bias
    hidden_f, pullback = jax.vjp(gelu_tanh, preact)
    hidden = hidden_f.astype(jnp.bfloat16)
    grad_pre = pullback(cotangent.astype(jnp.float32))[0]
    grad_rows_b = grad_pre.astype(jnp.bfloat16).reshape(tgt_blocks, block, width)
    grad_panel = partial_panel(0, tiles, tile_cols, live_mask, grad_rows_b, panel_blocks)
    for round_index in range(1, slot_count):
        outgoing = partial_panel(
            round_index, tiles, tile_cols, live_mask, grad_rows_b, panel_blocks
        )
        grad_panel = grad_panel + swapped(outgoing, "dom", top_bit - round_index)
    grad_proj = lax.psum_scatter(grad_panel, "rep", scatter_dimension=0, tiled=True).astype(
        jnp.bfloat16
    )
    weight_local = lax.dot_general(
        feats, grad_proj, (((0,), (0,)), ((), ())), preferred_element_type=jnp.float32
    )
    bias_local = jnp.sum(grad_pre, axis=0)
    grad_weight, grad_bias = lax.psum((weight_local, bias_local), ("dom", "rep"))
    grad_feats = lax.dot_general(
        grad_proj, weight, (((1,), (1,)), ((), ())), preferred_element_type=jnp.float32
    ).astype(jnp.bfloat16)
    return (hidden, grad_weight, grad_bias, grad_feats)


def solution(mesh):
    return jax.shard_map(
        body,
        mesh=mesh,
        in_specs=(
            P(("dom", "rep"), None),
            P(),
            P(),
            P(("dom", "rep"), None, None, None, None),
            P(("dom", "rep"), None, None),
            P(("dom", "rep"), None),
            P(("dom", "rep"), None),
        ),
        out_specs=(P(("dom", "rep"), None), P(), P(), P(("dom", "rep"), None)),
        check_vma=False,
    )
```

profile of v0, /device:TPU:1, one launch (start us, length us, event | category | flops | bytes accessed | tf_op | source)
XLA Modules:
  0.0 770.6 jit_solution(12770402989602264046)
XLA Ops:
  8.8 19.5 %all_gather.3 = bf16[1024,128]{1,0:T(8,128)(2,1)S(1)} all-gather(bf16[128,128]{1,0:T(8,128)(2,1)S(1)} %convolution_convert_fusion.1), channel_id=1, replica_groups=mesh['dom'=64,'rep'=8] {'rep'}, dimensions={0}, use_global_device_ids=true | all-gather | bytes 294912 | tf_op jit(solution)/shard_map/all_gather | solution.py:53
  32.2 8.4 %collective-permute-start.1 = (bf16[1024,128]{1,0:T(8,128)(2,1)S(1)}, bf16[1024,128]{1,0:T(8,128)(2,1)S(1)}, u32[]{:S(2)}, u32[]{:S(2)}) collective-permute-start(bf16[1024,128]{1,0:T(8,128)(2,1)S(1)} %all_gather.3), channel_id=1, source_target_pairs={{0,128},{8,136},{16,144},{24,152},{32,160},{40,168},{48,176},{56,1... | collective-permute-start | bytes 786440 | tf_op jit(solution)/shard_map/ppermute | solution.py:10
  40.6 7.9 %collective-permute-start = (bf16[1024,128]{1,0:T(8,128)(2,1)S(1)}, bf16[1024,128]{1,0:T(8,128)(2,1)S(1)}, u32[]{:S(2)}, u32[]{:S(2)}) collective-permute-start(bf16[1024,128]{1,0:T(8,128)(2,1)S(1)} %all_gather.3), channel_id=1, source_target_pairs={{0,256},{8,264},{16,272},{24,280},{32,288},{40,296},{48,304},{56,3... | collective-permute-start | bytes 786440 | tf_op jit(solution)/shard_map/ppermute | solution.py:10
  55.6 8.0 %collective-permute-done.2 = bf16[1024,128]{1,0:T(8,128)(2,1)S(1)} collective-permute-done((bf16[1024,128]{1,0:T(8,128)(2,1)S(1)}, bf16[1024,128]{1,0:T(8,128)(2,1)S(1)}, u32[]{:S(2)}, u32[]{:S(2)}) %collective-permute-start.2) | collective-permute-done | bytes 262176 | tf_op jit(solution)/shard_map/ppermute | solution.py:10
  66.0 19.9 %collective-permute-done.1 = bf16[1024,128]{1,0:T(8,128)(2,1)S(1)} collective-permute-done((bf16[1024,128]{1,0:T(8,128)(2,1)S(1)}, bf16[1024,128]{1,0:T(8,128)(2,1)S(1)}, u32[]{:S(2)}, u32[]{:S(2)}) %collective-permute-start.1) | collective-permute-done | bytes 262176 | tf_op jit(solution)/shard_map/ppermute | solution.py:10
  89.1 2.3 fusion.100
  91.4 3.2 fusion.12
  94.6 3.2 fusion.10
  97.8 2.0 fusion.8
  99.8 3.2 fusion.6
  103.0 4.6 scatter_fusion.1
  107.6 11.3 %collective-permute-start.4 = (f32[1024,128]{1,0:T(8,128)S(1)}, f32[1024,128]{1,0:T(8,128)}, u32[]{:S(2)}, u32[]{:S(2)}) collective-permute-start(f32[1024,128]{1,0:T(8,128)S(1)} %bitcast.141), channel_id=1, source_target_pairs={{0,256},{8,264},{16,272},{24,280},{32,288},{40,296},{48,304},{56,3... | collective-permute-start | bytes 1572872 | tf_op jit(solution)/shard_map/ppermute | solution.py:10
  118.9 4.6 scatter_fusion.2
  123.5 1.9 collective-permute-start.5
  125.5 2.6 scatter_fusion.3
  130.1 4.6 scatter_fusion.4
  134.7 1.9 collective-permute-start.7
  136.6 3.2 fusion.14
  139.9 4.6 scatter_fusion
  144.5 8.2 %collective-permute-done.4 = f32[1024,128]{1,0:T(8,128)} collective-permute-done((f32[1024,128]{1,0:T(8,128)S(1)}, f32[1024,128]{1,0:T(8,128)}, u32[]{:S(2)}, u32[]{:S(2)}) %collective-permute-start.4) | collective-permute-done | bytes 524320 | tf_op jit(solution)/shard_map/ppermute | solution.py:10
  152.6 51.6 %collective-permute-done.5 = f32[1024,128]{1,0:T(8,128)} collective-permute-done((f32[1024,128]{1,0:T(8,128)S(1)}, f32[1024,128]{1,0:T(8,128)}, u32[]{:S(2)}, u32[]{:S(2)}) %collective-permute-start.5) | collective-permute-done | bytes 524320 | tf_op jit(solution)/shard_map/ppermute | solution.py:10
  204.2 2.3 fusion.53
  206.5 114.1 %psum.15 = f32[128]{0:T(128)} all-reduce(f32[128]{0:T(128)S(1)} %get-tuple-element.8), channel_id=1, replica_groups=mesh['dom'=64,'rep'=8] {'dom','rep'}, use_global_device_ids=true, to_apply=%region_8.9 | all-reduce | flops 128 | bytes 1024 | tf_op jit(solution)/shard_map/psum | solution.py:78
  324.0 438.2 %all-reduce.2.cloned.1.call-done = f32[128,128]{0,1:T(8,128)} async-done(((f32[128,128]{0,1:T(8,128)}), f32[128,128]{0,1:T(8,128)}) %all-reduce.2.cloned.1.call-update) | async-done | bytes 65552 | tf_op jit(solution)/shard_map/psum | solution.py:78
  (47 shorter events, 24.9 us)
Async XLA Ops:
  7.2 0.8 copy-start
  7.2 313.5 %reduce-scatter.2.cloned.1.call-start = ((), (), s32[]{:S(2)}) async-start(), calls=%async_computation.1 | async-start | bytes 589824 | tf_op jit(solution)/shard_map/reduce_scatter | solution.py:71
  28.3 24.9 %collective-permute-start.3 = (bf16[1024,128]{1,0:T(8,128)(2,1)S(1)}, bf16[1024,128]{1,0:T(8,128)(2,1)S(1)}, u32[]{:S(2)}, u32[]{:S(2)}) collective-permute-start(bf16[1024,128]{1,0:T(8,128)(2,1)S(1)} %all_gather.3), channel_id=1, source_target_pairs={{0,32},{8,40},{16,48},{24,56},{32,0},{40,8},{48,16},{56,24},{64,96... | collective-permute-start | bytes 786440 | tf_op jit(solution)/shard_map/ppermute | solution.py:10
  30.2 33.4 %collective-permute-start.2 = (bf16[1024,128]{1,0:T(8,128)(2,1)S(1)}, bf16[1024,128]{1,0:T(8,128)(2,1)S(1)}, u32[]{:S(2)}, u32[]{:S(2)}) collective-permute-start(bf16[1024,128]{1,0:T(8,128)(2,1)S(1)} %all_gather.3), channel_id=1, source_target_pairs={{0,64},{8,72},{16,80},{24,88},{32,96},{40,104},{48,112},{56,120},{... | collective-permute-start | bytes 786440 | tf_op jit(solution)/shard_map/ppermute | solution.py:10
  32.2 53.7 %collective-permute-start.1 = (bf16[1024,128]{1,0:T(8,128)(2,1)S(1)}, bf16[1024,128]{1,0:T(8,128)(2,1)S(1)}, u32[]{:S(2)}, u32[]{:S(2)}) collective-permute-start(bf16[1024,128]{1,0:T(8,128)(2,1)S(1)} %all_gather.3), channel_id=1, source_target_pairs={{0,128},{8,136},{16,144},{24,152},{32,160},{40,168},{48,176},{56,1... | collective-permute-start | bytes 786440 | tf_op jit(solution)/shard_map/ppermute | solution.py:10
  40.6 47.7 %collective-permute-start = (bf16[1024,128]{1,0:T(8,128)(2,1)S(1)}, bf16[1024,128]{1,0:T(8,128)(2,1)S(1)}, u32[]{:S(2)}, u32[]{:S(2)}) collective-permute-start(bf16[1024,128]{1,0:T(8,128)(2,1)S(1)} %all_gather.3), channel_id=1, source_target_pairs={{0,256},{8,264},{16,272},{24,280},{32,288},{40,296},{48,304},{56,3... | collective-permute-start | bytes 786440 | tf_op jit(solution)/shard_map/ppermute | solution.py:10
  86.6 2.4 copy-start.2
  86.6 2.4 copy-start.3
  107.6 45.0 %collective-permute-start.4 = (f32[1024,128]{1,0:T(8,128)S(1)}, f32[1024,128]{1,0:T(8,128)}, u32[]{:S(2)}, u32[]{:S(2)}) collective-permute-start(f32[1024,128]{1,0:T(8,128)S(1)} %bitcast.141), channel_id=1, source_target_pairs={{0,256},{8,264},{16,272},{24,280},{32,288},{40,296},{48,304},{56,3... | collective-permute-start | bytes 1572872 | tf_op jit(solution)/shard_map/ppermute | solution.py:10
  123.5 80.7 %collective-permute-start.5 = (f32[1024,128]{1,0:T(8,128)S(1)}, f32[1024,128]{1,0:T(8,128)}, u32[]{:S(2)}, u32[]{:S(2)}) collective-permute-start(f32[1024,128]{1,0:T(8,128)S(1)} %bitcast.142), channel_id=1, source_target_pairs={{0,128},{8,136},{16,144},{24,152},{32,160},{40,168},{48,176},{56,1... | collective-permute-start | bytes 1572872 | tf_op jit(solution)/shard_map/ppermute | solution.py:10
  128.1 76.1 %collective-permute-start.6 = (f32[1024,128]{1,0:T(8,128)S(1)}, f32[1024,128]{1,0:T(8,128)S(1)}, u32[]{:S(2)}, u32[]{:S(2)}) collective-permute-start(f32[1024,128]{1,0:T(8,128)S(1)} %bitcast.143), channel_id=1, source_target_pairs={{0,64},{8,72},{16,80},{24,88},{32,96},{40,104},{48,112},{56,120},{... | collective-permute-start | bytes 1572872 | tf_op jit(solution)/shard_map/ppermute | solution.py:10
  134.7 69.5 %collective-permute-start.7 = (f32[1024,128]{1,0:T(8,128)S(1)}, f32[1024,128]{1,0:T(8,128)}, u32[]{:S(2)}, u32[]{:S(2)}) collective-permute-start(f32[1024,128]{1,0:T(8,128)S(1)} %bitcast.144), channel_id=1, source_target_pairs={{0,32},{8,40},{16,48},{24,56},{32,0},{40,8},{48,16},{56,24},{64,96... | collective-permute-start | bytes 1572872 | tf_op jit(solution)/shard_map/ppermute | solution.py:10
  144.4 177.9 %copy-start.1 = (bf16[128,128]{1,0:T(8,128)(2,1)S(1)}, bf16[128,128]{1,0:T(8,128)(2,1)}, u32[]{:S(2)}) copy-start(bf16[128,128]{1,0:T(8,128)(2,1)} %param.8) | copy-start | bytes 98308
  206.5 555.7 %all-reduce.2.cloned.1.call-start = ((), (), s32[]{:S(2)}) async-start(), calls=%async_computation.2 | async-start | bytes 131072 | tf_op jit(solution)/shard_map/psum | solution.py:78
Sparse Core Ops, SparseCore 0:
  206.6 44.0 reduce-scatter.1
  322.5 439.6 all-reduce.1
where the time goes:
time: 772 us; the launch traced here: 771 us
  waiting for transfers between devices  526 us (68%)
  blocking collectives  134 us (17%)
  starting transfers between devices  37.3 us (5%)
  matrix products  27.8 us (4%)
  other arithmetic  25.4 us (3%)
  between operations  14.3 us (2%)
    psum x1, waiting for transfers between devices, body(): lax.psum((weight_local, bias_local), ('dom', 'rep'))  438 us
    psum x1, blocking collectives, body(): lax.psum((weight_local, bias_local), ('dom', 'rep'))  114 us
    ppermute x8, waiting for transfers between devices, swapped(): return lax.ppermute(value, axis, pairs)  87.7 us
    ppermute x8, starting transfers between devices, swapped(): return lax.ppermute(value, axis, pairs)  37.2 us
    scatter-add x5, other arithmetic, partial_panel(): placed.at[targets]  20.9 us
    all_gather x1, blocking collectives, body(): own_rows = lax.all_gather(projected, 'rep', axis=0, tiled=True)  19.5 us
  transfers between devices with their start and end apart: 10, of which 5 were waited for; matrix products, arithmetic and copies ran while one was open for 4% of the time, Pallas kernels for 0%

commit v1 on v0

--- a/solution.py
+++ b/solution.py
@@ -75,7 +75,7 @@
         feats, grad_proj, (((0,), (0,)), ((), ())), preferred_element_type=jnp.float32
     )
     bias_local = jnp.sum(grad_pre, axis=0)
-    grad_weight, grad_bias = lax.psum((weight_local, bias_local), ("dom", "rep"))
+    grad_weight, grad_bias = lax.psum(lax.psum((weight_local, bias_local), "dom"), "rep")
     grad_feats = lax.dot_general(
         grad_proj, weight, (((1,), (1,)), ((), ())), preferred_element_type=jnp.float32
     ).astype(jnp.bfloat16)

time: 772 us -> 597 us (0.77)
  waiting for transfers between devices: 526 us -> 307 us
  blocking collectives: 134 us -> 178 us
    psum x1 -> x2, waiting for transfers between devices: 438 us -> 175 us  [the longest x1 95.5 us: body(): lax.psum((weight_local, bias_local), 'dom')]
    psum x1 -> x2, blocking collectives: 114 us -> 159 us  [the longest x1 116 us: body(): lax.psum((weight_local, bias_local), 'dom')]
    reduce_scatter x1, waiting for transfers between devices: 0.01 us -> 44.2 us  [body(): lax.psum_scatter(grad_panel, 'rep', scatter_dimension=0, tiled=True)]
  transfers between devices with their start and end apart: 10 -> 11, of which waited for: 5 -> 7; matrix products, arithmetic and copies ran while one was open for 4% -> 6% of each run, Pallas kernels for 0% -> 0%
where the time goes in v1:
time: 597 us; the launch traced here: 595 us
  waiting for transfers between devices  307 us (51%)
  blocking collectives  178 us (30%)
  starting transfers between devices  37.4 us (6%)
  matrix products  27.8 us (5%)
  other arithmetic  25.4 us (4%)
  between operations  14 us (2%)
  local copies, waits for them, and re-layouts  6.1 us (1%)
    psum x1, blocking collectives, body(): lax.psum((weight_local, bias_local), 'dom')  116 us
    psum x1, waiting for transfers between devices, body(): lax.psum((weight_local, bias_local), 'dom')  95.5 us
    ppermute x8, waiting for transfers between devices, swapped(): return lax.ppermute(value, axis, pairs)  87.7 us
    psum x1, waiting for transfers between devices, body(): lax.psum(lax.psum((weight_local, bias_local), 'dom'), 'rep')  79.1 us
    reduce_scatter x1, waiting for transfers between devices, body(): lax.psum_scatter(grad_panel, 'rep', scatter_dimension=0, tiled=True)  44.2 us
    psum x1, blocking collectives, body(): lax.psum(lax.psum((weight_local, bias_local), 'dom'), 'rep')  42.5 us
    ppermute x8, starting transfers between devices, swapped(): return lax.ppermute(value, axis, pairs)  37.2 us
    scatter-add x5, other arithmetic, partial_panel(): placed.at[targets]  20.9 us
  transfers between devices with their start and end apart: 11, of which 7 were waited for; matrix products, arithmetic and copies ran while one was open for 6% of the time, Pallas kernels for 0%

profile of v1, /device:TPU:1, one launch (start us, length us, event | category | flops | bytes accessed | tf_op | source)
XLA Modules:
  0.0 595.4 jit_solution(16742236536779313913)
XLA Ops:
  8.8 19.5 %all_gather.3 = bf16[1024,128]{1,0:T(8,128)(2,1)S(1)} all-gather(bf16[128,128]{1,0:T(8,128)(2,1)S(1)} %convolution_convert_fusion.1), channel_id=1, replica_groups=mesh['dom'=64,'rep'=8] {'rep'}, dimensions={0}, use_global_device_ids=true | all-gather | bytes 294912 | tf_op jit(solution)/shard_map/all_gather | solution.py:53
  32.2 8.4 %collective-permute-start.1 = (bf16[1024,128]{1,0:T(8,128)(2,1)S(1)}, bf16[1024,128]{1,0:T(8,128)(2,1)S(1)}, u32[]{:S(2)}, u32[]{:S(2)}) collective-permute-start(bf16[1024,128]{1,0:T(8,128)(2,1)S(1)} %all_gather.3), channel_id=1, source_target_pairs={{0,128},{8,136},{16,144},{24,152},{32,160},{40,168},{48,176},{56,1... | collective-permute-start | bytes 786440 | tf_op jit(solution)/shard_map/ppermute | solution.py:10
  40.6 7.9 %collective-permute-start = (bf16[1024,128]{1,0:T(8,128)(2,1)S(1)}, bf16[1024,128]{1,0:T(8,128)(2,1)S(1)}, u32[]{:S(2)}, u32[]{:S(2)}) collective-permute-start(bf16[1024,128]{1,0:T(8,128)(2,1)S(1)} %all_gather.3), channel_id=1, source_target_pairs={{0,256},{8,264},{16,272},{24,280},{32,288},{40,296},{48,304},{56,3... | collective-permute-start | bytes 786440 | tf_op jit(solution)/shard_map/ppermute | solution.py:10
  55.6 8.0 %collective-permute-done.2 = bf16[1024,128]{1,0:T(8,128)(2,1)S(1)} collective-permute-done((bf16[1024,128]{1,0:T(8,128)(2,1)S(1)}, bf16[1024,128]{1,0:T(8,128)(2,1)S(1)}, u32[]{:S(2)}, u32[]{:S(2)}) %collective-permute-start.2) | collective-permute-done | bytes 262176 | tf_op jit(solution)/shard_map/ppermute | solution.py:10
  66.0 19.9 %collective-permute-done.1 = bf16[1024,128]{1,0:T(8,128)(2,1)S(1)} collective-permute-done((bf16[1024,128]{1,0:T(8,128)(2,1)S(1)}, bf16[1024,128]{1,0:T(8,128)(2,1)S(1)}, u32[]{:S(2)}, u32[]{:S(2)}) %collective-permute-start.1) | collective-permute-done | bytes 262176 | tf_op jit(solution)/shard_map/ppermute | solution.py:10
  89.1 2.3 fusion.100
  91.4 3.2 fusion.12
  94.6 3.2 fusion.10
  99.8 3.2 fusion.6
  103.0 4.6 scatter_fusion.1
  107.6 11.3 %collective-permute-start.4 = (f32[1024,128]{1,0:T(8,128)S(1)}, f32[1024,128]{1,0:T(8,128)}, u32[]{:S(2)}, u32[]{:S(2)}) collective-permute-start(f32[1024,128]{1,0:T(8,128)S(1)} %bitcast.141), channel_id=1, source_target_pairs={{0,256},{8,264},{16,272},{24,280},{32,288},{40,296},{48,304},{56,3... | collective-permute-start | bytes 1572872 | tf_op jit(solution)/shard_map/ppermute | solution.py:10
  118.9 4.6 scatter_fusion.2
  125.5 2.6 scatter_fusion.3
  130.1 4.6 scatter_fusion.4
  136.6 3.2 fusion.14
  139.9 4.6 scatter_fusion
  144.5 8.2 %collective-permute-done.4 = f32[1024,128]{1,0:T(8,128)} collective-permute-done((f32[1024,128]{1,0:T(8,128)S(1)}, f32[1024,128]{1,0:T(8,128)}, u32[]{:S(2)}, u32[]{:S(2)}) %collective-permute-start.4) | collective-permute-done | bytes 524320 | tf_op jit(solution)/shard_map/ppermute | solution.py:10
  152.6 51.6 %collective-permute-done.5 = f32[1024,128]{1,0:T(8,128)} collective-permute-done((f32[1024,128]{1,0:T(8,128)S(1)}, f32[1024,128]{1,0:T(8,128)}, u32[]{:S(2)}, u32[]{:S(2)}) %collective-permute-start.5) | collective-permute-done | bytes 524320 | tf_op jit(solution)/shard_map/ppermute | solution.py:10
  204.2 2.3 fusion.53
  206.5 44.2 %reduce-scatter.2.cloned.1.call-done = f32[128,128]{1,0:T(8,128)} async-done(((f32[1024,128]{1,0:T(8,128)}), f32[128,128]{1,0:T(8,128)}) %reduce-scatter.2.cloned.1.call-update) | async-done | bytes 65552 | tf_op jit(solution)/shard_map/reduce_scatter | solution.py:71
  252.4 116.1 %psum.30 = f32[128]{0:T(128)S(1)} all-reduce(f32[128]{0:T(128)S(1)} %get-tuple-element.8), channel_id=1, replica_groups=mesh['dom'=64,'rep'=8] {'dom'}, use_global_device_ids=true, to_apply=%region_9.10 | all-reduce | flops 128 | bytes 1024 | tf_op jit(solution)/shard_map/psum | solution.py:78
  368.5 42.5 %psum.31 = f32[128]{0:T(128)} all-reduce(f32[128]{0:T(128)S(1)} %psum.30), channel_id=1, replica_groups=mesh['dom'=64,'rep'=8] {'rep'}, use_global_device_ids=true, to_apply=%region_10.11 | all-reduce | flops 128 | bytes 1024 | tf_op jit(solution)/shard_map/psum | solution.py:78
  411.1 95.5 %all-reduce.3.cloned.1.call-done = f32[128,128]{0,1:T(8,128)} async-done(((f32[128,128]{0,1:T(8,128)}), f32[128,128]{0,1:T(8,128)}) %all-reduce.3.cloned.1.call-update) | async-done | bytes 65552 | tf_op jit(solution)/shard_map/psum | solution.py:78
  508.2 79.1 %all-reduce.5.cloned.1.call-done = f32[128,128]{0,1:T(8,128)} async-done(((f32[128,128]{0,1:T(8,128)}), f32[128,128]{0,1:T(8,128)}) %all-reduce.5.cloned.1.call-update) | async-done | bytes 65552 | tf_op jit(solution)/shard_map/psum | solution.py:78
  (51 shorter events, 30.7 us)
Async XLA Ops:
  7.2 0.8 copy-start
  7.2 243.5 %reduce-scatter.2.cloned.1.call-start = ((), (), s32[]{:S(2)}) async-start(), calls=%async_computation.1 | async-start | bytes 589824 | tf_op jit(solution)/shard_map/reduce_scatter | solution.py:71
  28.3 24.9 %collective-permute-start.3 = (bf16[1024,128]{1,0:T(8,128)(2,1)S(1)}, bf16[1024,128]{1,0:T(8,128)(2,1)S(1)}, u32[]{:S(2)}, u32[]{:S(2)}) collective-permute-start(bf16[1024,128]{1,0:T(8,128)(2,1)S(1)} %all_gather.3), channel_id=1, source_target_pairs={{0,32},{8,40},{16,48},{24,56},{32,0},{40,8},{48,16},{56,24},{64,96... | collective-permute-start | bytes 786440 | tf_op jit(solution)/shard_map/ppermute | solution.py:10
  30.2 33.4 %collective-permute-start.2 = (bf16[1024,128]{1,0:T(8,128)(2,1)S(1)}, bf16[1024,128]{1,0:T(8,128)(2,1)S(1)}, u32[]{:S(2)}, u32[]{:S(2)}) collective-permute-start(bf16[1024,128]{1,0:T(8,128)(2,1)S(1)} %all_gather.3), channel_id=1, source_target_pairs={{0,64},{8,72},{16,80},{24,88},{32,96},{40,104},{48,112},{56,120},{... | collective-permute-start | bytes 786440 | tf_op jit(solution)/shard_map/ppermute | solution.py:10
  32.2 53.7 %collective-permute-start.1 = (bf16[1024,128]{1,0:T(8,128)(2,1)S(1)}, bf16[1024,128]{1,0:T(8,128)(2,1)S(1)}, u32[]{:S(2)}, u32[]{:S(2)}) collective-permute-start(bf16[1024,128]{1,0:T(8,128)(2,1)S(1)} %all_gather.3), channel_id=1, source_target_pairs={{0,128},{8,136},{16,144},{24,152},{32,160},{40,168},{48,176},{56,1... | collective-permute-start | bytes 786440 | tf_op jit(solution)/shard_map/ppermute | solution.py:10
  40.6 47.7 %collective-permute-start = (bf16[1024,128]{1,0:T(8,128)(2,1)S(1)}, bf16[1024,128]{1,0:T(8,128)(2,1)S(1)}, u32[]{:S(2)}, u32[]{:S(2)}) collective-permute-start(bf16[1024,128]{1,0:T(8,128)(2,1)S(1)} %all_gather.3), channel_id=1, source_target_pairs={{0,256},{8,264},{16,272},{24,280},{32,288},{40,296},{48,304},{56,3... | collective-permute-start | bytes 786440 | tf_op jit(solution)/shard_map/ppermute | solution.py:10
  86.6 2.4 copy-start.2
  86.6 2.4 copy-start.3
  107.6 45.0 %collective-permute-start.4 = (f32[1024,128]{1,0:T(8,128)S(1)}, f32[1024,128]{1,0:T(8,128)}, u32[]{:S(2)}, u32[]{:S(2)}) collective-permute-start(f32[1024,128]{1,0:T(8,128)S(1)} %bitcast.141), channel_id=1, source_target_pairs={{0,256},{8,264},{16,272},{24,280},{32,288},{40,296},{48,304},{56,3... | collective-permute-start | bytes 1572872 | tf_op jit(solution)/shard_map/ppermute | solution.py:10
  123.5 80.7 %collective-permute-start.5 = (f32[1024,128]{1,0:T(8,128)S(1)}, f32[1024,128]{1,0:T(8,128)}, u32[]{:S(2)}, u32[]{:S(2)}) collective-permute-start(f32[1024,128]{1,0:T(8,128)S(1)} %bitcast.142), channel_id=1, source_target_pairs={{0,128},{8,136},{16,144},{24,152},{32,160},{40,168},{48,176},{56,1... | collective-permute-start | bytes 1572872 | tf_op jit(solution)/shard_map/ppermute | solution.py:10
  128.1 76.1 %collective-permute-start.6 = (f32[1024,128]{1,0:T(8,128)S(1)}, f32[1024,128]{1,0:T(8,128)S(1)}, u32[]{:S(2)}, u32[]{:S(2)}) collective-permute-start(f32[1024,128]{1,0:T(8,128)S(1)} %bitcast.143), channel_id=1, source_target_pairs={{0,64},{8,72},{16,80},{24,88},{32,96},{40,104},{48,112},{56,120},{... | collective-permute-start | bytes 1572872 | tf_op jit(solution)/shard_map/ppermute | solution.py:10
  134.7 69.5 %collective-permute-start.7 = (f32[1024,128]{1,0:T(8,128)S(1)}, f32[1024,128]{1,0:T(8,128)}, u32[]{:S(2)}, u32[]{:S(2)}) collective-permute-start(f32[1024,128]{1,0:T(8,128)S(1)} %bitcast.144), channel_id=1, source_target_pairs={{0,32},{8,40},{16,48},{24,56},{32,0},{40,8},{48,16},{56,24},{64,96... | collective-permute-start | bytes 1572872 | tf_op jit(solution)/shard_map/ppermute | solution.py:10
  144.4 362.1 %copy-start.1 = (bf16[128,128]{1,0:T(8,128)(2,1)S(1)}, bf16[128,128]{1,0:T(8,128)(2,1)}, u32[]{:S(2)}) copy-start(bf16[128,128]{1,0:T(8,128)(2,1)} %param.8) | copy-start | bytes 98308
  206.5 300.0 %all-reduce.3.cloned.1.call-start = ((), (), s32[]{:S(2)}) async-start(), calls=%async_computation.2 | async-start | bytes 131072 | tf_op jit(solution)/shard_map/psum | solution.py:78
  252.4 334.9 %all-reduce.5.cloned.1.call-start = ((), (), s32[]{:S(2)}) async-start(), calls=%async_computation.3 | async-start | bytes 131072 | tf_op jit(solution)/shard_map/psum | solution.py:78
Sparse Core Ops, SparseCore 0:
  206.6 44.0 reduce-scatter.1
  254.7 251.7 all-reduce.2
  508.9 78.4 all-reduce.4
